TPU v7x, 256 devices: a whole 4x4x8 slice. The times are simulated.
256 devices in a mesh: dp: 16 (over x, y), tensor: 16 (over z, core).
Axes of the slice: x: 4, y: 4, z: 8, core: 2. Of those that a mesh axis runs over, the one named last changes fastest.
Arguments:
- hidden: bfloat16 [32768, 1280], P(('dp', 'tensor')), may hold values from -6 to 6
- lengths: int32 [16, 8], P('dp'), may hold values from 1 to 1024, 2048 in all within a row
- request_prompt: int32 [16, 8], P('dp'), may hold values from 0 to 31
- request_adapter: int32 [16, 8], P('dp'), may hold values from 0 to 63
- prompt_page_table: int32 [32, 4], replicated, may hold values from 0 to 63
- prefix_page_cache: bfloat16 [64, 64, 2048], P('dp', None, 'tensor'), may hold values from -6 to 6
- query_key_value_weight: bfloat16 [1280, 3072], P(None, 'tensor'), may hold values from -0.15625 to 0.15625
- adapter_down: bfloat16 [64, 1280, 16], P('dp'), may hold values from -0.15625 to 0.15625
- adapter_up: bfloat16 [64, 16, 3072], P('dp', None, 'tensor'), may hold values from -1.5 to 1.5
- attention_scale: float32 [1024], P('tensor'), may hold values from 0.5 to 1.5
- output_matrix: bfloat16 [1024, 1280], P('tensor'), may hold values from -0.1875 to 0.1875
- attention_rate: float32 [1280], replicated, may hold values from 0.05 to 0.5
- up_matrix: bfloat16 [1280, 5120], P(None, 'tensor'), may hold values from -0.15625 to 0.15625
- gate_matrix: bfloat16 [1280, 5120], P(None, 'tensor'), may hold values from -0.15625 to 0.15625
- up_scaling: float32 [5120], P('tensor'), may hold values from 0.5 to 2
- gate_scaling: float32 [5120], P('tensor'), may hold values from 0.5 to 2
- down_matrix: bfloat16 [5120, 1280], P('tensor'), may hold values from -0.078125 to 0.078125
- feedforward_rate: float32 [1280], replicated, may hold values from 0.05 to 0.5
Outputs:
- hidden_out: bfloat16 [32768, 1280], P(('dp', 'tensor'))
Inputs may be any that keep to these rules, and one draw needn't show every extreme that they name: Each group's lengths sum to 2048.
All inputs are finite; a program needn't handle non-finite values.
Results may differ from a plain program's by a relative error of at most 0.015.
Values may be sent and summed in bfloat16 or wider, within the bound.
A program may use at most 64 MiB of HBM per device.

v0:
```python
import math
import jax
import jax.numpy as jnp
from jax import lax
from jax.sharding import PartitionSpec as P

MODEL_WIDTH = 1280
HEAD_WIDTH = 64
ADAPTER_RANK = 16
GROUP_REQUESTS = 8
PAGE = 64
PREFIX_LEN = 256
adapter_scale = 0.5
epsilon = 1e-06


def renorm(matrix):
    return matrix * lax.rsqrt(jnp.mean(matrix * matrix, axis=-1, keepdims=True) + epsilon)


def to_unit(vectors):
    return vectors * lax.rsqrt(jnp.sum(vectors * vectors, axis=-1, keepdims=True) + epsilon)


def rotate(vectors, position):
    half_size = vectors.shape[-1] // 2
    frequency = jnp.exp(
        jnp.arange(half_size).astype(jnp.float32) * (-2.0 * math.log(10000.0) / vectors.shape[-1])
    )
    angles = position[:, None] * frequency[None, :]
    cosine = jnp.cos(angles)[:, None, :]
    sines = jnp.sin(angles)[:, None, :]
    first_half = vectors[..., :half_size]
    second_half = vectors[..., half_size:]
    return jnp.concatenate(
        [first_half * cosine - second_half * sines, first_half * sines + second_half * cosine],
        axis=-1,
    )


def layout(counts, total_rows):
    row_ends = jnp.cumsum(counts)
    starts = row_ends - counts
    row_ids = jnp.arange(total_rows, dtype=jnp.int32)
    request_number = jnp.sum((row_ids[:, None] >= row_ends[None, :]).astype(jnp.int32), axis=1)
    selected_adapter = (
        request_number[:, None] == jnp.arange(counts.shape[0], dtype=jnp.int32)[None, :]
    )
    offset = row_ids - jnp.sum(jnp.where(selected_adapter, starts[None, :], 0), axis=1)
    return (request_number, offset)


def attend(queries, key_all, value_all, request_number, key_request, key_row):
    rows_total = queries.shape[0]
    block_rows = min(512, rows_total)
    score_scale = math.sqrt(queries.shape[-1])
    row_ids = jnp.arange(rows_total, dtype=jnp.int32)

    def one_block(block_index):
        first_row = block_index * block_rows
        query_block = lax.dynamic_slice_in_dim(queries, first_row, block_rows, 0)
        request_block = lax.dynamic_slice_in_dim(request_number, first_row, block_rows, 0)
        row_block = lax.dynamic_slice_in_dim(row_ids, first_row, block_rows, 0)
        scores = (
            jnp.einsum("qhd,khd->hqk", query_block, key_all, preferred_element_type=jnp.float32)
            * score_scale
        )
        allowed = (request_block[:, None] == key_request[None, :]) & (
            key_row[None, :] <= row_block[:, None]
        )
        exp_scores = jnp.where(allowed[None], jnp.exp(scores), 0.0)
        weights = (exp_scores / jnp.sum(exp_scores, axis=-1, keepdims=True)).astype(jnp.bfloat16)
        mixed_block = jnp.einsum(
            "hqk,khd->qhd", weights, value_all, preferred_element_type=jnp.float32
        )
        return mixed_block.reshape(block_rows, -1).astype(jnp.bfloat16)

    blocks = lax.map(one_block, jnp.arange(rows_total // block_rows, dtype=jnp.int32))
    return blocks.reshape(rows_total, -1)


def hidden_units(row_values, up_matrix, gate_matrix, up_scaling, gate_scaling):
    up_part = jnp.dot(row_values, up_matrix, preferred_element_type=jnp.float32) * up_scaling
    gate_part = jnp.dot(row_values, gate_matrix, preferred_element_type=jnp.float32) * gate_scaling
    return (up_part * jax.nn.silu(gate_part)).astype(jnp.bfloat16)


def local(
    hidden,
    lengths,
    request_prompt,
    request_adapter,
    prompt_page_table,
    prefix_page_cache,
    query_key_value_weight,
    adapter_down,
    adapter_up,
    attention_scale,
    output_matrix,
    attention_rate,
    up_matrix,
    gate_matrix,
    up_scaling,
    gate_scaling,
    down_matrix,
    feedforward_rate,
):
    tok_rows = hidden.shape[0]
    group_rows = tok_rows * lax.axis_size("tensor")
    heads_here = query_key_value_weight.shape[1] // (3 * HEAD_WIDTH)
    gain_qk = attention_scale.reshape(heads_here, HEAD_WIDTH)
    request_number, offset = layout(lengths[0], group_rows)
    position = offset.astype(jnp.float32) + PREFIX_LEN
    local_cache = prefix_page_cache.reshape(
        prefix_page_cache.shape[0], PAGE, heads_here, 2, HEAD_WIDTH
    )
    local_keys = (to_unit(local_cache[:, :, :, 0, :].astype(jnp.float32)) * gain_qk).astype(
        jnp.bfloat16
    )
    prepared = jnp.stack([local_keys, local_cache[:, :, :, 1, :]], axis=3).reshape(
        prefix_page_cache.shape
    )
    all_pages = lax.all_gather(prepared, "dp", axis=0, tiled=True)
    down_all, up_all = (
        lax.all_gather(adapter_down, "dp", axis=0, tiled=True),
        lax.all_gather(adapter_up, "dp", axis=0, tiled=True),
    )
    every_row = lax.all_gather(hidden, "tensor", axis=0, tiled=True)
    adapter_count = down_all.shape[0]
    onehot = (
        request_adapter[0][:, None] == jnp.arange(adapter_count, dtype=jnp.int32)[None, :]
    ).astype(jnp.bfloat16)
    selected_down = jnp.dot(
        onehot, down_all.reshape(adapter_count, -1), preferred_element_type=jnp.float32
    ).astype(jnp.bfloat16)
    selected_down = jnp.transpose(
        selected_down.reshape(GROUP_REQUESTS, MODEL_WIDTH, ADAPTER_RANK), (1, 0, 2)
    ).reshape(MODEL_WIDTH, GROUP_REQUESTS * ADAPTER_RANK)
    selected_up = jnp.dot(
        onehot, up_all.reshape(adapter_count, -1), preferred_element_type=jnp.float32
    ).astype(jnp.bfloat16)
    selected_up = selected_up.reshape(GROUP_REQUESTS * ADAPTER_RANK, heads_here * 3 * HEAD_WIDTH)
    request_of_slot = jnp.arange(GROUP_REQUESTS * ADAPTER_RANK, dtype=jnp.int32) // ADAPTER_RANK
    plain_projection = jnp.dot(
        every_row, query_key_value_weight, preferred_element_type=jnp.float32
    )
    adapter_middle = jnp.dot(every_row, selected_down, preferred_element_type=jnp.float32)
    adapter_middle = jnp.where(
        request_number[:, None] == request_of_slot[None, :], adapter_middle, 0.0
    ).astype(jnp.bfloat16)
    query_key_value = (
        plain_projection
        + adapter_scale * jnp.dot(adapter_middle, selected_up, preferred_element_type=jnp.float32)
    ).reshape(group_rows, heads_here, 3, HEAD_WIDTH)
    queries = (to_unit(rotate(query_key_value[:, :, 0, :], position)) * gain_qk).astype(
        jnp.bfloat16
    )
    key_own = (to_unit(rotate(query_key_value[:, :, 1, :], position)) * gain_qk).astype(
        jnp.bfloat16
    )
    value_own = query_key_value[:, :, 2, :].astype(jnp.bfloat16)
    page_list = prompt_page_table[request_prompt[0]].reshape(-1)
    picked = jnp.take(all_pages, page_list, axis=0).reshape(
        GROUP_REQUESTS * PREFIX_LEN, heads_here, 2, HEAD_WIDTH
    )
    key_all = jnp.concatenate([picked[:, :, 0, :], key_own], axis=0)
    value_all = jnp.concatenate([picked[:, :, 1, :], value_own], axis=0)
    key_request = jnp.concatenate(
        [jnp.arange(GROUP_REQUESTS * PREFIX_LEN, dtype=jnp.int32) // PREFIX_LEN, request_number],
        axis=0,
    )
    key_row = jnp.concatenate(
        [
            jnp.full((GROUP_REQUESTS * PREFIX_LEN,), -1, jnp.int32),
            jnp.arange(group_rows, dtype=jnp.int32),
        ],
        axis=0,
    )
    attn = attend(queries, key_all, value_all, request_number, key_request, key_row)
    attn_sum = lax.psum_scatter(
        jnp.dot(attn, output_matrix, preferred_element_type=jnp.float32).astype(jnp.bfloat16),
        "tensor",
        scatter_dimension=0,
        tiled=True,
    ).astype(jnp.float32)
    base_rows = hidden.astype(jnp.float32)
    mixed = renorm(base_rows + attention_rate * (renorm(attn_sum) - base_rows)).astype(jnp.bfloat16)
    unit_values = hidden_units(
        lax.all_gather(mixed, "tensor", axis=0, tiled=True),
        up_matrix,
        gate_matrix,
        up_scaling,
        gate_scaling,
    )
    mlp_sum = lax.psum_scatter(
        jnp.dot(unit_values, down_matrix, preferred_element_type=jnp.float32).astype(jnp.bfloat16),
        "tensor",
        scatter_dimension=0,
        tiled=True,
    ).astype(jnp.float32)
    mixed_rows = mixed.astype(jnp.float32)
    return renorm(mixed_rows + feedforward_rate * (renorm(mlp_sum) - mixed_rows)).astype(
        jnp.bfloat16
    )


def solution(mesh):
    placed = (
        P(("dp", "tensor"), None),
        P("dp", None),
        P("dp", None),
        P("dp", None),
        P(),
        P("dp", None, "tensor"),
        P(None, "tensor"),
        P("dp", None, None),
        P("dp", None, "tensor"),
        P("tensor"),
        P("tensor", None),
        P(),
        P(None, "tensor"),
        P(None, "tensor"),
        P("tensor"),
        P("tensor"),
        P("tensor", None),
        P(),
    )
    return jax.shard_map(
        local, mesh=mesh, in_specs=placed, out_specs=P(("dp", "tensor"), None), check_vma=False
    )
```

profile of v0, /device:TPU:8, one launch (start us, length us, event | category | flops | bytes accessed | tf_op | source)
XLA Modules:
  0.0 397.9 jit_solution(10989033186772423542)
XLA Ops:
  6.5 1.0 reshape.596
  7.6 0.6 multiply_reduce_fusion.4
  8.2 0.1 slice.53
  8.3 1.0 multiply_convert_fusion.4
  9.3 0.4 pad_maximum_fusion.4
  9.7 0.7 reshape.597
  10.5 0.7 all-gather.7.cloned.1.call-update
  11.3 0.7 all-gather.5.cloned.1.call-update
  12.0 0.8 copy.41
  12.8 0.7 fusion.40
  13.4 0.6 gather_fusion
  14.0 0.1 reshape.598
  14.1 0.1 reshape.595
  14.1 0.8 reduce-window.4
  15.0 24.1 %all_gather.17 = bf16[64,16,192]{2,1,0:T(8,128)(2,1)S(1)} all-gather(bf16[4,16,192]{2,1,0:T(8,128)(2,1)} %param.28), channel_id=1, replica_groups=mesh['dp'=16,'tensor'=16] {'dp'}, dimensions={0}, use_global_device_ids=true | all-gather | bytes 417792 | tf_op jit(solution)/shard_map/all_gather | solution.py:126
  39.1 0.5 reshape.591
  39.6 0.9 convolution_convert_fusion.3
  40.5 0.1 reshape.592
  40.7 0.1 broadcast_in_dim.45
  40.9 0.1 convert_reduce_fusion
  41.0 0.7 fusion.42
  41.6 0.1 select_reduce_fusion
  41.7 19.0 %all-gather.9.cloned.1.call-done = bf16[64,64,128]{2,1,0:T(8,128)(2,1)} async-done(((bf16[4,64,128]{2,1,0:T(8,128)(2,1)}), bf16[64,64,128]{2,1,0:T(8,128)(2,1)}) %all-gather.9.cloned.1.call-update) | async-done | bytes 1048592 | tf_op jit(solution)/shard_map/all_gather | solution.py:123
  60.8 1.9 gather_fusion.1
  62.7 0.4 reshape.616
  63.1 0.9 copy.44
  64.1 0.9 slice_bitcast_fusion.2
  64.9 49.1 %all-gather.7.cloned.1.call-done = bf16[64,1280,16]{1,2,0:T(8,128)(2,1)} async-done(((bf16[4,1280,16]{1,2,0:T(8,128)(2,1)}), bf16[64,1280,16]{1,2,0:T(8,128)(2,1)}) %all-gather.7.cloned.1.call-update) | async-done | bytes 2621456 | tf_op jit(solution)/shard_map/all_gather | solution.py:125
  114.0 9.7 %copy.39 = bf16[64,1280,16]{0,2,1:T(8,128)(2,1)} copy(bf16[64,1280,16]{1,2,0:T(8,128)(2,1)} %all-gather.7.cloned.1.call-done) | data formatting | bytes 5242880 | tf_op jit(solution)/shard_map/all_gather | solution.py:125
  123.7 4.7 %convolution_convert_fusion = bf16[8,20480]{1,0:T(8,128)(2,1)} fusion(bf16[64,20480]{0,1:T(8,128)(2,1)} %bitcast.89, s32[8]{0:T(128)S(1)} %bitcast.97), kind=kOutput, calls=%fused_computation.13 | convolution fusion | flops 21135872 | bytes 2949152 | tf_op jit(solution)/shard_map/dot_general | solution.py:133
  128.4 2.9 reshape.589
  131.3 1.6 copy.40
  132.9 26.0 %all-gather.5.cloned.1.call-done = bf16[2048,1280]{1,0:T(8,128)(2,1)} async-done(((bf16[128,1280]{1,0:T(8,128)(2,1)}), bf16[2048,1280]{1,0:T(8,128)(2,1)}) %all-gather.5.cloned.1.call-update) | async-done | bytes 5242896 | tf_op jit(solution)/shard_map/all_gather | solution.py:128
  158.9 5.6 %fusion.46 = f32[2048,192]{0,1:T(8,128)} fusion(bf16[2048,1280]{1,0:T(8,128)(2,1)} %all-gather.5.cloned.1.call-done, bf16[1280,192]{0,1:T(8,128)(2,1)} %param.26), kind=kOutput, calls=%fused_computation.120 | convolution fusion | flops 1006632960 | bytes 7307264 | tf_op jit(solution)/shard_map/dot_general | solution.py:144
  164.6 5.0 %fusion.11 = f32[2048,192]{0,1:T(8,128)S(1)} fusion(f32[2048,192]{0,1:T(8,128)} %fusion.46, bf16[128,192]{1,0:T(8,128)(2,1)S(1)} %reshape.592, bf16[1280,128]{0,1:T(8,128)(2,1)S(1)} %bitcast.94, bf16[2048,1280]{1,0:T(8,128)(2,1)} %all-gather.5.cloned.1.call-done, s32[2048]{0:T(1024)S(1)} %convert_reduce_fusion, s32[128]{0:T(128)S(1)} %and_select_fusion), kind=kOutput, calls=%fused_computation.22 | convolution fusion | flops 773324800 | bytes 8774144 | tf_op jit(solution)/shard_map/dot_general | solution.py:153
  169.7 1.2 fusion.32
  171.0 0.1 multiply_reduce_fusion.2
  171.1 0.2 multiply_convert_fusion.2
  171.5 22.6 %while.11 = (s32[]{:T(128)}, bf16[4,512,64]{1,2,0:T(8,128)(2,1)S(1)}, s32[4]{0:T(128)S(1)}, s32[2048]{0:T(1024)S(1)}, s32[4096]{0:T(1024)S(1)}, /*index=5*/s32[2...) while((s32[]{:T(128)}, ...), condition=%wide.region_8.9_spmd, body=%wide.region_6.8_spmd.sunk | while | flops 553680384 | bytes 18006224 | solution.py:78
  171.5 0.6 dynamic_slice.32
  172.7 0.1 dynamic_slice.33
  172.9 2.7 fusion.65
  175.5 1.5 fusion.66
  177.1 0.6 dynamic_slice.32
  178.5 2.7 fusion.65
  181.1 1.5 fusion.66
  182.7 0.6 dynamic_slice.32
  184.1 2.7 fusion.65
  186.7 1.5 fusion.66
  188.3 0.6 dynamic_slice.32
  189.7 2.7 fusion.65
  192.3 1.5 fusion.66
  194.1 3.9 convolution_convert_fusion.2
  198.1 63.4 %reduce-scatter.3.cloned.1.call-done = bf16[128,1280]{1,0:T(8,128)(2,1)} async-done(((bf16[2048,1280]{1,0:T(8,128)(2,1)}), bf16[128,1280]{1,0:T(8,128)(2,1)}) %reduce-scatter.3.cloned.1.call-update) | async-done | bytes 327696 | tf_op jit(solution)/shard_map/reduce_scatter | solution.py:180
  261.5 1.1 fusion.16
  262.6 1.3 multiply_reduce_fusion.1
  264.0 2.1 multiply_convert_fusion.1
  266.1 42.1 %all-gather.11.cloned.1.call-done = bf16[2048,1280]{1,0:T(8,128)(2,1)} async-done(((bf16[128,1280]{1,0:T(8,128)(2,1)}), bf16[2048,1280]{1,0:T(8,128)(2,1)}) %all-gather.11.cloned.1.call-update) | async-done | bytes 5242896 | tf_op jit(solution)/shard_map/all_gather | solution.py:189
  308.2 5.9 %convolution_multiply_fusion = f32[2048,320]{0,1:T(8,128)} fusion(bf16[2048,1280]{1,0:T(8,128)(2,1)} %all-gather.11.cloned.1.call-done, bf16[1280,320]{0,1:T(8,128)(2,1)S(1)} %copy-done.12, f32[320]{0:T(512)S(1)} %copy-done.14), kind=kOutput, calls=%fused_computation.17 | convolution fusion | flops 1678376960 | bytes 8684800 | tf_op jit(solution)/shard_map/dot_general | solution.py:84
  314.1 8.7 %convolution_convert_fusion.1 = bf16[2048,1280]{1,0:T(8,128)(2,1)} fusion(bf16[320,1280]{1,0:T(8,128)(2,1)S(1)} %copy-done, bf16[2048,1280]{1,0:T(8,128)(2,1)} %all-gather.11.cloned.1.call-done, bf16[1280,320]{0,1:T(8,128)(2,1)S(1)} %copy-done.13, f32[2048,320]{0,1:T(8,128)} %convolution_multiply_fusion, f32[320]{0:T(512)S(1)} %copy-done.15), kind=kOutput, calls=%fused_computation.14 | convolution fusion | flops 3362652160 | bytes 14746880 | tf_op jit(solution)/shard_map/dot_general | solution.py:196
  322.9 63.6 %reduce-scatter.5.cloned.1.call-done = bf16[128,1280]{1,0:T(8,128)(2,1)} async-done(((bf16[2048,1280]{1,0:T(8,128)(2,1)}), bf16[128,1280]{1,0:T(8,128)(2,1)}) %reduce-scatter.5.cloned.1.call-update) | async-done | bytes 327696 | tf_op jit(solution)/shard_map/reduce_scatter | solution.py:195
  386.5 1.1 fusion.18
  387.6 1.3 multiply_reduce_fusion
  389.0 2.1 multiply_convert_fusion
  (77 shorter events, 1.3 us)
Async XLA Ops:
  6.5 307.6 %copy-start = (bf16[320,1280]{1,0:T(8,128)(2,1)S(1)}, bf16[320,1280]{1,0:T(8,128)(2,1)}, u32[]{:S(2)}) copy-start(bf16[320,1280]{1,0:T(8,128)(2,1)} %param.36) | copy-start | bytes 2457604
  6.5 54.2 %all-gather.9.cloned.1.call-start = ((), (), s32[]{:S(2)}) async-start(), calls=%async_computation.4 | async-start | bytes 1114112 | tf_op jit(solution)/shard_map/all_gather | solution.py:123
  10.5 103.5 %all-gather.7.cloned.1.call-start = ((), (), s32[]{:S(2)}) async-start(), calls=%async_computation.3 | async-start | bytes 2785280 | tf_op jit(solution)/shard_map/all_gather | solution.py:125
  11.2 147.7 %all-gather.5.cloned.1.call-start = ((), (), s32[]{:S(2)}) async-start(), calls=%async_computation.2 | async-start | bytes 5570560 | tf_op jit(solution)/shard_map/all_gather | solution.py:128
  12.0 249.5 %reduce-scatter.3.cloned.1.call-start = ((), (), s32[]{:S(2)}) async-start(), calls=%async_computation.5 | async-start | bytes 5570560 | tf_op jit(solution)/shard_map/reduce_scatter | solution.py:180
  64.0 59.7 %copy-start.11 = (s32[1,8]{1,0:T(1,128)S(1)}, s32[1,8]{1,0:T(1,128)}, u32[]{:S(2)}) copy-start(s32[1,8]{1,0:T(1,128)} %param.23) | copy-start | bytes 100
  132.9 31.6 %copy-start.3 = (bf16[1280,8,16]{0,2,1:T(8,128)(2,1)S(1)}, bf16[1280,8,16]{0,2,1:T(8,128)(2,1)}, u32[]{:S(2)}) copy-start(bf16[1280,8,16]{0,2,1:T(8,128)(2,1)} %copy.40) | copy-start | bytes 983044
  164.6 6.5 %copy-start.10 = (f32[64]{0:T(128)S(1)}, f32[64]{0:T(128)}, u32[]{:S(2)}) copy-start(f32[64]{0:T(128)} %param.29) | copy-start | bytes 772
  169.6 1.7 copy-start.5
  169.6 1.8 copy-start.4
  169.6 1.8 copy-start.6
  169.6 1.8 copy-start.16
  171.4 22.7 %copy-start.7 = (bf16[64,1280]{1,0:T(8,128)(2,1)S(1)}, bf16[64,1280]{1,0:T(8,128)(2,1)}, u32[]{:S(2)}) copy-start(bf16[64,1280]{1,0:T(8,128)(2,1)} %param.30) | copy-start | bytes 491524
  198.0 64.6 %copy-start.2 = (bf16[128,1280]{1,0:T(8,128)(2,1)S(1)}, bf16[128,1280]{1,0:T(8,128)(2,1)}, u32[]{:S(2)}) copy-start(bf16[128,1280]{1,0:T(8,128)(2,1)} %param.20) | copy-start | bytes 983044
  198.0 64.6 %copy-start.8 = (f32[1280]{0:T(1024)S(1)}, f32[1280]{0:T(1024)}, u32[]{:S(2)}) copy-start(f32[1280]{0:T(1024)} %param.31) | copy-start | bytes 15364
  198.0 110.2 %copy-start.12 = (bf16[1280,320]{0,1:T(8,128)(2,1)S(1)}, bf16[1280,320]{0,1:T(8,128)(2,1)}, u32[]{:S(2)}) copy-start(bf16[1280,320]{0,1:T(8,128)(2,1)} %param.33) | copy-start | bytes 2457604
  198.0 110.2 %copy-start.14 = (f32[320]{0:T(512)S(1)}, f32[320]{0:T(512)}, u32[]{:S(2)}) copy-start(f32[320]{0:T(512)} %param.35) | copy-start | bytes 3844
  198.0 110.2 %all-gather.11.cloned.1.call-start = ((), (), s32[]{:S(2)}) async-start(), calls=%async_computation.6 | async-start | bytes 5570560 | tf_op jit(solution)/shard_map/all_gather | solution.py:189
  266.1 48.1 %copy-start.13 = (bf16[1280,320]{0,1:T(8,128)(2,1)S(1)}, bf16[1280,320]{0,1:T(8,128)(2,1)}, u32[]{:S(2)}) copy-start(bf16[1280,320]{0,1:T(8,128)(2,1)} %param.32) | copy-start | bytes 2457604
  266.1 48.0 %copy-start.15 = (f32[320]{0:T(512)S(1)}, f32[320]{0:T(512)}, u32[]{:S(2)}) copy-start(f32[320]{0:T(512)} %param.34) | copy-start | bytes 3844
  266.1 120.4 %reduce-scatter.5.cloned.1.call-start = ((), (), s32[]{:S(2)}) async-start(), calls=%async_computation.7 | async-start | bytes 5570560 | tf_op jit(solution)/shard_map/reduce_scatter | solution.py:195
  322.8 64.8 %copy-start.1 = (bf16[128,1280]{1,0:T(8,128)(2,1)S(1)}, bf16[128,1280]{1,0:T(8,128)(2,1)}, u32[]{:S(2)}) copy-start(bf16[128,1280]{1,0:T(8,128)(2,1)} %multiply_convert_fusion.1) | copy-start | bytes 983044
  322.8 64.8 %copy-start.9 = (f32[1280]{0:T(1024)S(1)}, f32[1280]{0:T(1024)}, u32[]{:S(2)}) copy-start(f32[1280]{0:T(1024)} %param.37) | copy-start | bytes 15364
Sparse Core Ops, SparseCore 0:
  10.6 50.1 all-gather.8
  63.3 50.6 all-gather.6
  115.8 43.0 all-gather.4
  198.1 63.3 reduce-scatter.2
  266.2 41.9 all-gather.10
  323.0 63.4 reduce-scatter.4
where the time goes:
time: 399 us; the launch traced here: 398 us
  waiting for transfers between devices  265 us (66%)
  matrix products  51.4 us (13%)
  local copies, waits for them, and re-layouts  25.6 us (6%)
  blocking collectives  24.1 us (6%)
  other arithmetic  15.1 us (4%)
  between operations  13.9 us (3%)
    reduce_scatter x1, waiting for transfers between devices, local(): lax.psum_scatter(jnp.dot(unit_values, down_matrix, preferred_element_type...  63.6 us
    reduce_scatter x1, waiting for transfers between devices, local(): lax.psum_scatter(jnp.dot(attn, output_matrix, preferred_element_type=jnp....  63.4 us
    all_gather x1, waiting for transfers between devices, local(): lax.all_gather(adapter_down, 'dp', axis=0, tiled=True)  49.1 us
    all_gather x1, waiting for transfers between devices, local(): lax.all_gather(mixed, 'tensor', axis=0, tiled=True)  42.1 us
    all_gather x1, waiting for transfers between devices, local(): every_row = lax.all_gather(hidden, 'tensor', axis=0, tiled=True)  26 us
    all_gather x1, blocking collectives, local(): lax.all_gather(adapter_up, 'dp', axis=0, tiled=True)  24.1 us
    all_gather x1, waiting for transfers between devices, local(): all_pages = lax.all_gather(prepared, 'dp', axis=0, tiled=True)  19 us
    dot_general x4, matrix products, one_block(): jnp.einsum('qhd,khd->hqk', query_block, key_all, preferred_element_type=j...  10.7 us
  transfers between devices with their start and end apart: 6, of which 6 were waited for; matrix products, arithmetic and copies ran while one was open for 7% of the time, Pallas kernels for 0%

commit v1 on v0

--- a/solution.py
+++ b/solution.py
@@ -12,6 +12,27 @@
 PREFIX_LEN = 256
 adapter_scale = 0.5
 epsilon = 1e-06
+
+
+def gather_around(array, axis, dim):
+    size, index, extent = (lax.axis_size(axis), lax.axis_index(axis), array.shape[dim])
+    ahead = [(i, (i + 1) % size) for i in range(size)]
+    backward = [(i, (i - 1) % size) for i in range(size)]
+    whole = jnp.zeros((*array.shape[:dim], size * extent, *array.shape[dim + 1 :]), array.dtype)
+    whole = lax.dynamic_update_slice_in_dim(whole, array, index * extent, axis=dim)
+    from_left = from_right = array
+    half = size // 2
+    for step in range(1, half + 1):
+        from_left = lax.ppermute(from_left, axis, ahead)
+        whole = lax.dynamic_update_slice_in_dim(
+            whole, from_left, (index - step) % size * extent, axis=dim
+        )
+        if step < size - half:
+            from_right = lax.ppermute(from_right, axis, backward)
+            whole = lax.dynamic_update_slice_in_dim(
+                whole, from_right, (index + step) % size * extent, axis=dim
+            )
+    return whole
 
 
 def renorm(matrix):
@@ -125,7 +146,7 @@
         lax.all_gather(adapter_down, "dp", axis=0, tiled=True),
         lax.all_gather(adapter_up, "dp", axis=0, tiled=True),
     )
-    every_row = lax.all_gather(hidden, "tensor", axis=0, tiled=True)
+    every_row = gather_around(hidden, "tensor", 0)
     adapter_count = down_all.shape[0]
     onehot = (
         request_adapter[0][:, None] == jnp.arange(adapter_count, dtype=jnp.int32)[None, :]

time: 399 us -> 371 us (0.930)
  waiting for transfers between devices: 265 us -> 200 us
  starting transfers between devices: 0.2 us -> 23.8 us
  local copies, waits for them, and re-layouts: 25.6 us -> 40.5 us
    all_gather x1, waiting for transfers between devices: 49.1 us -> 8.76 us  [local(): lax.all_gather(adapter_down, 'dp', axis=0, tiled=True)]
    all_gather x1 -> x0, waiting for transfers between devices: 26 us -> none  [local(): every_row = lax.all_gather(hidden, 'tensor', axis=0, tiled=True)]
    ppermute x0 -> x15, starting transfers between devices: none -> 23.6 us  [the longest x7 23.6 us: gather_around(): from_right = lax.ppermute(from_right, axis, backward)]
    ppermute x0 -> x15, waiting for transfers between devices: none -> 21.3 us  [the longest x8 21.1 us: gather_around(): from_left = lax.ppermute(from_left, axis, ahead)]
    all_gather x1, waiting for transfers between devices: 19 us -> 0.01 us  [local(): all_pages = lax.all_gather(prepared, 'dp', axis=0, tiled=True)]
    dynamic_update_slice x0 -> x16, local copies, waits for them, and re-layouts: none -> 13 us  [the longest x7 6.2 us: gather_around(): lax.dynamic_update_slice_in_dim(whole, from_right, (index + step) % size...]
  transfers between devices with their start and end apart: 6 -> 20, of which waited for: 6 -> 11; matrix products, arithmetic and copies ran while one was open for 7% -> 7% of each run, Pallas kernels for 0% -> 0%
where the time goes in v1:
time: 371 us; the launch traced here: 370 us
  waiting for transfers between devices  200 us (54%)
  matrix products  49.3 us (13%)
  local copies, waits for them, and re-layouts  40.5 us (11%)
  blocking collectives  24 us (6%)
  starting transfers between devices  23.8 us (6%)
  other arithmetic  15.9 us (4%)
  between operations  13.9 us (4%)
    reduce_scatter x1, waiting for transfers between devices, local(): lax.psum_scatter(jnp.dot(attn, output_matrix, preferred_element_type=jnp....  64.7 us
    reduce_scatter x1, waiting for transfers between devices, local(): lax.psum_scatter(jnp.dot(unit_values, down_matrix, preferred_element_type...  63.5 us
    all_gather x1, waiting for transfers between devices, local(): lax.all_gather(mixed, 'tensor', axis=0, tiled=True)  41.9 us
    all_gather x1, blocking collectives, local(): lax.all_gather(adapter_up, 'dp', axis=0, tiled=True)  24 us
    ppermute x7, starting transfers between devices, gather_around(): from_right = lax.ppermute(from_right, axis, backward)  23.6 us
    ppermute x8, waiting for transfers between devices, gather_around(): from_left = lax.ppermute(from_left, axis, ahead)  21.1 us
    dot_general x4, matrix products, one_block(): jnp.einsum('qhd,khd->hqk', query_block, key_all, preferred_element_type=j...  10.7 us
    all_gather x1, local copies, waits for them, and re-layouts, local(): lax.all_gather(adapter_down, 'dp', axis=0, tiled=True)  9.71 us
  transfers between devices with their start and end apart: 20, of which 11 were waited for; matrix products, arithmetic and copies ran while one was open for 7% of the time, Pallas kernels for 0%

profile of v1, /device:TPU:8, one launch (start us, length us, event | category | flops | bytes accessed | tf_op | source)
XLA Modules:
  0.0 370.5 jit_solution(18183507783349604898)
XLA Ops:
  6.5 1.0 reshape.596
  8.4 1.0 multiply_convert_fusion.4
  9.7 0.7 reshape.597
  10.6 5.3 %collective-permute-start.1 = (bf16[128,1280]{1,0:T(8,128)(2,1)}, bf16[128,1280]{1,0:T(8,128)(2,1)S(1)}, u32[]{:S(2)}, u32[]{:S(2)}) collective-permute-start(bf16[128,1280]{1,0:T(8,128)(2,1)} %param.20), channel_id=1, source_target_pairs={{0,15},{1,0},{2,1},{3,2},{4,3},{5,4},{6,5},{7,6},{8,7},{9,8},{10,9... | collective-permute-start | bytes 983048 | tf_op jit(solution)/shard_map/ppermute | solution.py:31
  16.2 0.8 copy.41
  18.4 0.8 reduce-window.4
  19.3 24.0 %all_gather.13 = bf16[64,16,192]{2,1,0:T(8,128)(2,1)S(1)} all-gather(bf16[4,16,192]{2,1,0:T(8,128)(2,1)} %param.28), channel_id=1, replica_groups=mesh['dp'=16,'tensor'=16] {'dp'}, dimensions={0}, use_global_device_ids=true | all-gather | bytes 417792 | tf_op jit(solution)/shard_map/all_gather | solution.py:147
  43.8 0.9 convolution_convert_fusion.3
  45.9 2.6 broadcast_in_dim.41
  49.3 3.0 collective-permute-start.3
  52.2 0.8 constant_dynamic-update-slice_fusion.14
  53.0 0.7 constant_dynamic-update-slice_fusion.13
  53.7 3.2 collective-permute-done.2
  57.0 3.0 collective-permute-start.5
  59.9 0.8 constant_dynamic-update-slice_fusion.12
  61.4 3.2 collective-permute-done.4
  64.7 3.0 collective-permute-start.7
  67.6 0.8 constant_dynamic-update-slice_fusion.10
  68.4 0.8 constant_dynamic-update-slice_fusion.9
  69.2 3.2 collective-permute-done.6
  72.4 3.0 collective-permute-start.9
  76.1 0.7 constant_dynamic-update-slice_fusion.7
  76.8 3.3 collective-permute-done.8
  80.1 3.4 collective-permute-start.11
  83.5 0.8 constant_dynamic-update-slice_fusion.6
  85.0 2.8 collective-permute-done.10
  88.1 3.1 collective-permute-start.13
  91.2 0.8 constant_dynamic-update-slice_fusion.4
  92.7 1.9 gather_fusion.1
  95.0 0.9 copy.44
  95.9 0.9 broadcast_select_fusion
  96.8 0.7 constant_dynamic-update-slice_fusion.2
  97.5 1.7 constant_dynamic-update-slice_fusion.1
  99.2 5.2 %collective-permute-done.14 = bf16[128,1280]{1,0:T(8,128)(2,1)S(1)} collective-permute-done((bf16[128,1280]{1,0:T(8,128)(2,1)S(1)}, bf16[128,1280]{1,0:T(8,128)(2,1)S(1)}, u32[]{:S(2)}, u32[]{:S(2)}) %collective-permute-start.14) | collective-permute-done | bytes 327712 | tf_op jit(solution)/shard_map/ppermute | solution.py:26
  104.5 0.8 constant_dynamic-update-slice_fusion
  105.2 8.8 %all-gather.4.cloned.1.call-done = bf16[64,1280,16]{1,2,0:T(8,128)(2,1)} async-done(((bf16[4,1280,16]{1,2,0:T(8,128)(2,1)}), bf16[64,1280,16]{1,2,0:T(8,128)(2,1)}) %all-gather.4.cloned.1.call-update) | async-done | bytes 2621456 | tf_op jit(solution)/shard_map/all_gather | solution.py:146
  114.0 9.7 %copy.39 = bf16[64,1280,16]{0,2,1:T(8,128)(2,1)} copy(bf16[64,1280,16]{1,2,0:T(8,128)(2,1)} %all-gather.4.cloned.1.call-done) | data formatting | bytes 5242880 | tf_op jit(solution)/shard_map/all_gather | solution.py:146
  123.7 4.7 %convolution_convert_fusion = bf16[8,20480]{1,0:T(8,128)(2,1)} fusion(bf16[64,20480]{0,1:T(8,128)(2,1)} %bitcast.81, s32[8]{0:T(128)S(1)} %bitcast.89), kind=kOutput, calls=%fused_computation.13 | convolution fusion | flops 21135872 | bytes 2949152 | tf_op jit(solution)/shard_map/dot_general | solution.py:154
  128.4 2.9 reshape.589
  131.3 1.6 copy.40
  133.0 4.1 %convolution_multiply_fusion.2 = f32[2048,192]{0,1:T(8,128)S(1)} fusion(bf16[128,192]{1,0:T(8,128)(2,1)S(1)} %reshape.592, bf16[2048,1280]{1,0:T(8,128)(2,1)} %constant_dynamic-update-slice_fusion, bf16[1280,128]{0,1:T(8,128)(2,1)} %bitcast.86, s32[128]{0:T(128)S(1)} %and_select_fusion, s32[2048]{0:T(1024)S(1)} %convert_reduce_fusion), kind=kOutput, calls=%fused_computation.21 | convolution fusion | flops 772931584 | bytes 7201280 | tf_op jit(solution)/shard_map/dot_general | solution.py:174
  137.1 4.4 %convolution_add_fusion = f32[2048,192]{0,1:T(8,128)S(1)} fusion(f32[2048,192]{0,1:T(8,128)S(1)} %convolution_multiply_fusion.2, bf16[2048,1280]{1,0:T(8,128)(2,1)} %constant_dynamic-update-slice_fusion, bf16[1280,192]{0,1:T(8,128)(2,1)S(1)} %copy-done.5), kind=kOutput, calls=%fused_computation.22 | convolution fusion | flops 1007026176 | bytes 8880128 | tf_op jit(solution)/shard_map/dot_general | solution.py:165
  141.7 1.2 fusion.30
  143.4 22.6 %while.11 = (s32[]{:T(128)}, bf16[4,512,64]{1,2,0:T(8,128)(2,1)S(1)}, s32[4]{0:T(128)S(1)}, s32[2048]{0:T(1024)S(1)}, s32[4096]{0:T(1024)S(1)}, /*index=5*/s32[2...) while((s32[]{:T(128)}, ...), condition=%wide.region_8.9_spmd, body=%wide.region_6.8_spmd.sunk | while | flops 553680384 | bytes 18006224 | solution.py:99
  144.8 2.7 fusion.62
  147.5 1.5 fusion.63
  150.4 2.7 fusion.62
  153.1 1.5 fusion.63
  156.0 2.7 fusion.62
  158.7 1.5 fusion.63
  161.6 2.7 fusion.62
  164.3 1.5 fusion.63
  166.1 3.9 %convolution_convert_fusion.2 = bf16[2048,1280]{1,0:T(8,128)(2,1)} fusion(bf16[2048,64]{0,1:T(8,128)(2,1)S(1)} %bitcast.85, bf16[64,1280]{1,0:T(8,128)(2,1)S(1)} %copy-done.7), kind=kOutput, calls=%fused_computation.15 | convolution fusion | flops 338165760 | bytes 5668864 | tf_op jit(solution)/shard_map/dot_general | solution.py:202
  170.0 64.7 %reduce-scatter.3.cloned.1.call-done = bf16[128,1280]{1,0:T(8,128)(2,1)} async-done(((bf16[2048,1280]{1,0:T(8,128)(2,1)}), bf16[128,1280]{1,0:T(8,128)(2,1)}) %reduce-scatter.3.cloned.1.call-update) | async-done | bytes 327696 | tf_op jit(solution)/shard_map/reduce_scatter | solution.py:201
  234.7 1.1 fusion.14
  235.9 1.3 multiply_reduce_fusion.1
  237.2 2.1 multiply_convert_fusion.1
  239.4 41.9 %all-gather.8.cloned.1.call-done = bf16[2048,1280]{1,0:T(8,128)(2,1)} async-done(((bf16[128,1280]{1,0:T(8,128)(2,1)}), bf16[2048,1280]{1,0:T(8,128)(2,1)}) %all-gather.8.cloned.1.call-update) | async-done | bytes 5242896 | tf_op jit(solution)/shard_map/all_gather | solution.py:210
  281.2 5.9 %convolution_multiply_fusion = f32[2048,320]{0,1:T(8,128)} fusion(bf16[2048,1280]{1,0:T(8,128)(2,1)} %all-gather.8.cloned.1.call-done, bf16[1280,320]{0,1:T(8,128)(2,1)S(1)} %copy-done.12, f32[320]{0:T(512)S(1)} %copy-done.14), kind=kOutput, calls=%fused_computation.17 | convolution fusion | flops 1678376960 | bytes 8684800 | tf_op jit(solution)/shard_map/dot_general | solution.py:105
  287.2 8.7 %convolution_convert_fusion.1 = bf16[2048,1280]{1,0:T(8,128)(2,1)} fusion(bf16[320,1280]{1,0:T(8,128)(2,1)S(1)} %copy-done, bf16[2048,1280]{1,0:T(8,128)(2,1)} %all-gather.8.cloned.1.call-done, bf16[1280,320]{0,1:T(8,128)(2,1)S(1)} %copy-done.13, f32[2048,320]{0,1:T(8,128)} %convolution_multiply_fusion, f32[320]{0:T(512)S(1)} %copy-done.15), kind=kOutput, calls=%fused_computation.14 | convolution fusion | flops 3362652160 | bytes 14746880 | tf_op jit(solution)/shard_map/dot_general | solution.py:217
  295.9 63.5 %reduce-scatter.5.cloned.1.call-done = bf16[128,1280]{1,0:T(8,128)(2,1)} async-done(((bf16[2048,1280]{1,0:T(8,128)(2,1)}), bf16[128,1280]{1,0:T(8,128)(2,1)}) %reduce-scatter.5.cloned.1.call-update) | async-done | bytes 327696 | tf_op jit(solution)/shard_map/reduce_scatter | solution.py:216
  359.4 1.1 fusion.16
  360.6 1.3 multiply_reduce_fusion
  361.9 2.1 multiply_convert_fusion
  (120 shorter events, 12.5 us)
Async XLA Ops:
  6.5 280.7 %copy-start = (bf16[320,1280]{1,0:T(8,128)(2,1)S(1)}, bf16[320,1280]{1,0:T(8,128)(2,1)}, u32[]{:S(2)}) copy-start(bf16[320,1280]{1,0:T(8,128)(2,1)} %param.36) | copy-start | bytes 2457604
  6.5 42.0 %copy-start.2 = (bf16[128,1280]{1,0:T(8,128)(2,1)S(1)}, bf16[128,1280]{1,0:T(8,128)(2,1)}, u32[]{:S(2)}) copy-start(bf16[128,1280]{1,0:T(8,128)(2,1)} %param.20) | copy-start | bytes 983044
  6.5 86.1 %all-gather.6.cloned.1.call-start = ((), (), s32[]{:S(2)}) async-start(), calls=%async_computation.3 | async-start | bytes 1114112 | tf_op jit(solution)/shard_map/all_gather | solution.py:144
  10.5 103.5 %all-gather.4.cloned.1.call-start = ((), (), s32[]{:S(2)}) async-start(), calls=%async_computation.2 | async-start | bytes 2785280 | tf_op jit(solution)/shard_map/all_gather | solution.py:146
  10.5 38.7 %collective-permute-start = (bf16[128,1280]{1,0:T(8,128)(2,1)}, bf16[128,1280]{1,0:T(8,128)(2,1)S(1)}, u32[]{:S(2)}, u32[]{:S(2)}) collective-permute-start(bf16[128,1280]{1,0:T(8,128)(2,1)} %param.20), channel_id=1, source_target_pairs={{0,1},{1,2},{2,3},{3,4},{4,5},{5,6},{6,7},{7,8},{8,9},{9,10},{10,1... | collective-permute-start | bytes 983048 | tf_op jit(solution)/shard_map/ppermute | solution.py:26
  10.6 38.7 %collective-permute-start.1 = (bf16[128,1280]{1,0:T(8,128)(2,1)}, bf16[128,1280]{1,0:T(8,128)(2,1)S(1)}, u32[]{:S(2)}, u32[]{:S(2)}) collective-permute-start(bf16[128,1280]{1,0:T(8,128)(2,1)} %param.20), channel_id=1, source_target_pairs={{0,15},{1,0},{2,1},{3,2},{4,3},{5,4},{6,5},{7,6},{8,7},{9,8},{10,9... | collective-permute-start | bytes 983048 | tf_op jit(solution)/shard_map/ppermute | solution.py:31
  15.9 218.8 %reduce-scatter.3.cloned.1.call-start = ((), (), s32[]{:S(2)}) async-start(), calls=%async_computation.4 | async-start | bytes 5570560 | tf_op jit(solution)/shard_map/reduce_scatter | solution.py:201
  49.3 7.7 %collective-permute-start.2 = (bf16[128,1280]{1,0:T(8,128)(2,1)S(1)}, bf16[128,1280]{1,0:T(8,128)(2,1)S(1)}, u32[]{:S(2)}, u32[]{:S(2)}) collective-permute-start(bf16[128,1280]{1,0:T(8,128)(2,1)S(1)} %collective-permute-done), channel_id=1, source_target_pairs={{0,1},{1,2},{2,3},{3,4},{4,5},{5,6},{6,7},{7,8},{8,9},{9,10},{10,1... | collective-permute-start | bytes 983048 | tf_op jit(solution)/shard_map/ppermute | solution.py:26
  49.3 7.7 %collective-permute-start.3 = (bf16[128,1280]{1,0:T(8,128)(2,1)S(1)}, bf16[128,1280]{1,0:T(8,128)(2,1)S(1)}, u32[]{:S(2)}, u32[]{:S(2)}) collective-permute-start(bf16[128,1280]{1,0:T(8,128)(2,1)S(1)} %collective-permute-done.1), channel_id=1, source_target_pairs={{0,15},{1,0},{2,1},{3,2},{4,3},{5,4},{6,5},{7,6},{8,7},{9,8},{10,9... | collective-permute-start | bytes 983048 | tf_op jit(solution)/shard_map/ppermute | solution.py:31
  57.0 7.7 %collective-permute-start.4 = (bf16[128,1280]{1,0:T(8,128)(2,1)S(1)}, bf16[128,1280]{1,0:T(8,128)(2,1)S(1)}, u32[]{:S(2)}, u32[]{:S(2)}) collective-permute-start(bf16[128,1280]{1,0:T(8,128)(2,1)S(1)} %collective-permute-done.2), channel_id=1, source_target_pairs={{0,1},{1,2},{2,3},{3,4},{4,5},{5,6},{6,7},{7,8},{8,9},{9,10},{10,1... | collective-permute-start | bytes 983048 | tf_op jit(solution)/shard_map/ppermute | solution.py:26
  57.0 7.7 %collective-permute-start.5 = (bf16[128,1280]{1,0:T(8,128)(2,1)S(1)}, bf16[128,1280]{1,0:T(8,128)(2,1)S(1)}, u32[]{:S(2)}, u32[]{:S(2)}) collective-permute-start(bf16[128,1280]{1,0:T(8,128)(2,1)S(1)} %collective-permute-done.3), channel_id=1, source_target_pairs={{0,15},{1,0},{2,1},{3,2},{4,3},{5,4},{6,5},{7,6},{8,7},{9,8},{10,9... | collective-permute-start | bytes 983048 | tf_op jit(solution)/shard_map/ppermute | solution.py:31
  64.7 7.7 %collective-permute-start.6 = (bf16[128,1280]{1,0:T(8,128)(2,1)S(1)}, bf16[128,1280]{1,0:T(8,128)(2,1)S(1)}, u32[]{:S(2)}, u32[]{:S(2)}) collective-permute-start(bf16[128,1280]{1,0:T(8,128)(2,1)S(1)} %collective-permute-done.4), channel_id=1, source_target_pairs={{0,1},{1,2},{2,3},{3,4},{4,5},{5,6},{6,7},{7,8},{8,9},{9,10},{10,1... | collective-permute-start | bytes 983048 | tf_op jit(solution)/shard_map/ppermute | solution.py:26
  64.7 7.7 %collective-permute-start.7 = (bf16[128,1280]{1,0:T(8,128)(2,1)S(1)}, bf16[128,1280]{1,0:T(8,128)(2,1)S(1)}, u32[]{:S(2)}, u32[]{:S(2)}) collective-permute-start(bf16[128,1280]{1,0:T(8,128)(2,1)S(1)} %collective-permute-done.5), channel_id=1, source_target_pairs={{0,15},{1,0},{2,1},{3,2},{4,3},{5,4},{6,5},{7,6},{8,7},{9,8},{10,9... | collective-permute-start | bytes 983048 | tf_op jit(solution)/shard_map/ppermute | solution.py:31
  72.4 7.7 %collective-permute-start.8 = (bf16[128,1280]{1,0:T(8,128)(2,1)S(1)}, bf16[128,1280]{1,0:T(8,128)(2,1)S(1)}, u32[]{:S(2)}, u32[]{:S(2)}) collective-permute-start(bf16[128,1280]{1,0:T(8,128)(2,1)S(1)} %collective-permute-done.6), channel_id=1, source_target_pairs={{0,1},{1,2},{2,3},{3,4},{4,5},{5,6},{6,7},{7,8},{8,9},{9,10},{10,1... | collective-permute-start | bytes 983048 | tf_op jit(solution)/shard_map/ppermute | solution.py:26
  72.4 7.7 %collective-permute-start.9 = (bf16[128,1280]{1,0:T(8,128)(2,1)S(1)}, bf16[128,1280]{1,0:T(8,128)(2,1)S(1)}, u32[]{:S(2)}, u32[]{:S(2)}) collective-permute-start(bf16[128,1280]{1,0:T(8,128)(2,1)S(1)} %collective-permute-done.7), channel_id=1, source_target_pairs={{0,15},{1,0},{2,1},{3,2},{4,3},{5,4},{6,5},{7,6},{8,7},{9,8},{10,9... | collective-permute-start | bytes 983048 | tf_op jit(solution)/shard_map/ppermute | solution.py:31
  80.1 7.7 %collective-permute-start.10 = (bf16[128,1280]{1,0:T(8,128)(2,1)S(1)}, bf16[128,1280]{1,0:T(8,128)(2,1)S(1)}, u32[]{:S(2)}, u32[]{:S(2)}) collective-permute-start(bf16[128,1280]{1,0:T(8,128)(2,1)S(1)} %collective-permute-done.8), channel_id=1, source_target_pairs={{0,1},{1,2},{2,3},{3,4},{4,5},{5,6},{6,7},{7,8},{8,9},{9,10},{10,1... | collective-permute-start | bytes 983048 | tf_op jit(solution)/shard_map/ppermute | solution.py:26
  80.1 7.9 %collective-permute-start.11 = (bf16[128,1280]{1,0:T(8,128)(2,1)S(1)}, bf16[128,1280]{1,0:T(8,128)(2,1)S(1)}, u32[]{:S(2)}, u32[]{:S(2)}) collective-permute-start(bf16[128,1280]{1,0:T(8,128)(2,1)S(1)} %collective-permute-done.9), channel_id=1, source_target_pairs={{0,15},{1,0},{2,1},{3,2},{4,3},{5,4},{6,5},{7,6},{8,7},{9,8},{10,9... | collective-permute-start | bytes 983048 | tf_op jit(solution)/shard_map/ppermute | solution.py:31
  87.8 8.9 %collective-permute-start.12 = (bf16[128,1280]{1,0:T(8,128)(2,1)S(1)}, bf16[128,1280]{1,0:T(8,128)(2,1)S(1)}, u32[]{:S(2)}, u32[]{:S(2)}) collective-permute-start(bf16[128,1280]{1,0:T(8,128)(2,1)S(1)} %collective-permute-done.10), channel_id=1, source_target_pairs={{0,1},{1,2},{2,3},{3,4},{4,5},{5,6},{6,7},{7,8},{8,9},{9,10},{10,1... | collective-permute-start | bytes 983048 | tf_op jit(solution)/shard_map/ppermute | solution.py:26
  88.1 9.5 %collective-permute-start.13 = (bf16[128,1280]{1,0:T(8,128)(2,1)S(1)}, bf16[128,1280]{1,0:T(8,128)(2,1)}, u32[]{:S(2)}, u32[]{:S(2)}) collective-permute-start(bf16[128,1280]{1,0:T(8,128)(2,1)S(1)} %collective-permute-done.11), channel_id=1, source_target_pairs={{0,15},{1,0},{2,1},{3,2},{4,3},{5,4},{6,5},{7,6},{8,7},{9,8},{10,9... | collective-permute-start | bytes 983048 | tf_op jit(solution)/shard_map/ppermute | solution.py:31
  95.9 27.8 %copy-start.11 = (s32[1,8]{1,0:T(1,128)S(1)}, s32[1,8]{1,0:T(1,128)}, u32[]{:S(2)}) copy-start(s32[1,8]{1,0:T(1,128)} %param.23) | copy-start | bytes 100
  96.8 7.7 %collective-permute-start.14 = (bf16[128,1280]{1,0:T(8,128)(2,1)S(1)}, bf16[128,1280]{1,0:T(8,128)(2,1)S(1)}, u32[]{:S(2)}, u32[]{:S(2)}) collective-permute-start(bf16[128,1280]{1,0:T(8,128)(2,1)S(1)} %collective-permute-done.12), channel_id=1, source_target_pairs={{0,1},{1,2},{2,3},{3,4},{4,5},{5,6},{6,7},{7,8},{8,9},{9,10},{10,1... | collective-permute-start | bytes 983048 | tf_op jit(solution)/shard_map/ppermute | solution.py:26
  133.0 4.1 %copy-start.5 = (bf16[1280,192]{0,1:T(8,128)(2,1)S(1)}, bf16[1280,192]{0,1:T(8,128)(2,1)}, u32[]{:S(2)}) copy-start(bf16[1280,192]{0,1:T(8,128)(2,1)} %param.26) | copy-start | bytes 1474564
  137.1 4.5 %copy-start.4 = (bf16[2048,1,2,64]{0,3,2,1:T(8,128)(2,1)S(1)}, bf16[2048,1,2,64]{0,3,2,1:T(8,128)(2,1)}, u32[]{:S(2)}) copy-start(bf16[2048,1,2,64]{0,3,2,1:T(8,128)(2,1)} %broadcast_select_fusion) | copy-start | bytes 1572868
  141.5 1.6 copy-start.10
  141.5 1.9 copy-start.6
  141.5 1.9 copy-start.16
  143.4 22.7 %copy-start.7 = (bf16[64,1280]{1,0:T(8,128)(2,1)S(1)}, bf16[64,1280]{1,0:T(8,128)(2,1)}, u32[]{:S(2)}) copy-start(bf16[64,1280]{1,0:T(8,128)(2,1)} %param.30) | copy-start | bytes 491524
  169.9 65.9 %copy-start.3 = (bf16[128,1280]{1,0:T(8,128)(2,1)S(1)}, bf16[128,1280]{1,0:T(8,128)(2,1)}, u32[]{:S(2)}) copy-start(bf16[128,1280]{1,0:T(8,128)(2,1)} %param.20) | copy-start | bytes 983044
  169.9 65.9 %copy-start.8 = (f32[1280]{0:T(1024)S(1)}, f32[1280]{0:T(1024)}, u32[]{:S(2)}) copy-start(f32[1280]{0:T(1024)} %param.31) | copy-start | bytes 15364
  169.9 111.3 %copy-start.12 = (bf16[1280,320]{0,1:T(8,128)(2,1)S(1)}, bf16[1280,320]{0,1:T(8,128)(2,1)}, u32[]{:S(2)}) copy-start(bf16[1280,320]{0,1:T(8,128)(2,1)} %param.33) | copy-start | bytes 2457604
  169.9 111.3 %copy-start.14 = (f32[320]{0:T(512)S(1)}, f32[320]{0:T(512)}, u32[]{:S(2)}) copy-start(f32[320]{0:T(512)} %param.35) | copy-start | bytes 3844
  170.0 111.3 %all-gather.8.cloned.1.call-start = ((), (), s32[]{:S(2)}) async-start(), calls=%async_computation.5 | async-start | bytes 5570560 | tf_op jit(solution)/shard_map/all_gather | solution.py:210
  239.3 47.9 %copy-start.13 = (bf16[1280,320]{0,1:T(8,128)(2,1)S(1)}, bf16[1280,320]{0,1:T(8,128)(2,1)}, u32[]{:S(2)}) copy-start(bf16[1280,320]{0,1:T(8,128)(2,1)} %param.32) | copy-start | bytes 2457604
  239.3 47.9 %copy-start.15 = (f32[320]{0:T(512)S(1)}, f32[320]{0:T(512)}, u32[]{:S(2)}) copy-start(f32[320]{0:T(512)} %param.34) | copy-start | bytes 3844
  239.3 120.1 %reduce-scatter.5.cloned.1.call-start = ((), (), s32[]{:S(2)}) async-start(), calls=%async_computation.6 | async-start | bytes 5570560 | tf_op jit(solution)/shard_map/reduce_scatter | solution.py:216
  295.9 64.6 %copy-start.1 = (bf16[128,1280]{1,0:T(8,128)(2,1)S(1)}, bf16[128,1280]{1,0:T(8,128)(2,1)}, u32[]{:S(2)}) copy-start(bf16[128,1280]{1,0:T(8,128)(2,1)} %multiply_convert_fusion.1) | copy-start | bytes 983044
  295.9 64.6 %copy-start.9 = (f32[1280]{0:T(1024)S(1)}, f32[1280]{0:T(1024)}, u32[]{:S(2)}) copy-start(f32[1280]{0:T(1024)} %param.37) | copy-start | bytes 15364
Sparse Core Ops, SparseCore 0:
  10.6 50.1 all-gather.5
  63.3 50.6 all-gather.3
  170.1 64.5 reduce-scatter.2
  239.4 41.7 all-gather.7
  296.1 63.3 reduce-scatter.4
